TPU v7x, 256 devices: a whole 4x4x8 slice. The times are simulated.
256 devices in a mesh: req: 4 (over x_hi, core), tp: 64 (over z, x_lo, y).
Axes of the slice: x: 4 (x_hi: 2, x_lo: 2; x = x_hi * 2 + x_lo), y: 4, z: 8, core: 2. Of those that a mesh axis runs over, the one named last changes fastest.
Arguments:
- hidden: bfloat16 [4096, 8192], P('req', 'tp'), may hold values from -6 to 6
- query_weight: bfloat16 [8192, 8192], P(None, 'tp'), may hold values from -0.0625 to 0.0625
- key_value_weight: bfloat16 [8192, 2048], P(None, 'tp'), may hold values from -0.0625 to 0.0625
- adapter_down_maps: bfloat16 [64, 8192, 32], P('req', 'tp'), may hold values from -0.0625 to 0.0625
- adapter_up_maps: bfloat16 [64, 32, 8192], P('req', None, 'tp'), may hold values from -1 to 1
- token_request_start: int32 [4096], P('req'), may hold values from 0 to 31, as said below
- adapter_per_block: int32 [32], P('req'), may hold values from 0 to 63
Outputs:
- context: bfloat16 [4096, 8192], P('req', 'tp')
Inputs may be any that keep to these rules, and one draw needn't show every extreme that they name: `token_request_start`: each run of 1024 tokens along the req split holds whole requests; a request is a run of whole blocks of 128 tokens; the last block of each such run is a request of its own.
All inputs are finite; a program needn't handle non-finite values.
Results may differ from a plain program's by a relative error of at most 0.012.
Values may be sent and summed in bfloat16 or wider, within the bound.
No kernel may reach another device: no remote copies, remote signals or barrier semaphores. Data moves between devices by JAX's collectives and lax.ppermute only.
A program may use at most 64 MiB of HBM per device.

v0:
```python
import math
import jax
import jax.numpy as jnp
from jax import lax
from jax.sharding import PartitionSpec as P

HEAD_SIZE = 128
BLOCK = 128
ROPE_BASE = 500000.0
ADAPTER_SCALE = 2.0


def from_partner(block, axis, bit):
    count = lax.axis_size(axis)
    route = []
    for low in range(count):
        high = low | 1 << bit
        if high != low and high < count:
            route += [(low, high), (high, low)]
    return lax.ppermute(block, axis, route)


def rotate(vectors, positions):
    half_width = vectors.shape[-1] // 2
    steps_half = jnp.arange(half_width, dtype=jnp.float32)
    inverse = jnp.exp(-(2.0 * steps_half / vectors.shape[-1]) * math.log(ROPE_BASE))
    angles = positions.astype(jnp.float32)[:, None] * inverse[None, :]
    cosines = jnp.cos(angles)
    sines = jnp.sin(angles)
    front_half = vectors[:, :half_width]
    back_half = vectors[:, half_width:]
    return jnp.concatenate(
        [front_half * cosines - back_half * sines, back_half * cosines + front_half * sines], axis=1
    )


def attend(queries, key_rows, value_rows, request):
    group_rows = queries.shape[0]
    block_rows = min(512, group_rows)
    block_total = group_rows // block_rows
    places = jnp.arange(group_rows, dtype=jnp.int32)
    score_scale = 1.0 / math.sqrt(queries.shape[1])

    def one_block(block_index):
        begin_row = block_index * block_rows
        q_blk = lax.dynamic_slice_in_dim(queries, begin_row, block_rows, 0)
        r_blk = lax.dynamic_slice_in_dim(request, begin_row, block_rows, 0)
        p_blk = lax.dynamic_slice_in_dim(places, begin_row, block_rows, 0)
        scores = (
            lax.dot_general(
                q_blk, key_rows, (((1,), (1,)), ((), ())), preferred_element_type=jnp.float32
            )
            * score_scale
        )
        allowed = (r_blk[:, None] == request[None, :]) & (places[None, :] <= p_blk[:, None])
        scores = jnp.where(allowed, scores, jnp.float32(-1e30))
        row_max = jnp.max(scores, axis=1, keepdims=True)
        weights = jnp.exp(scores - row_max)
        probs = (weights / jnp.sum(weights, axis=1, keepdims=True)).astype(jnp.bfloat16)
        return jnp.dot(probs, value_rows, preferred_element_type=jnp.float32).astype(jnp.bfloat16)

    blocks = lax.map(one_block, jnp.arange(block_total, dtype=jnp.int32))
    return blocks.reshape(group_rows, value_rows.shape[1])


def body(
    hidden,
    query_weight,
    key_value_weight,
    adapter_down_maps,
    adapter_up_maps,
    token_request_start,
    adapter_per_block,
):
    group_rows = hidden.shape[0]
    local_width = hidden.shape[1]
    head_cols = query_weight.shape[1]
    kv_cols = key_value_weight.shape[1]
    device = lax.axis_index("tp")
    spread = 2 * HEAD_SIZE // kv_cols
    piece = lax.all_gather(hidden, "tp", axis=1, tiled=True)
    query_total = jnp.dot(piece, query_weight, preferred_element_type=jnp.float32)
    kv_sum = jnp.dot(piece, key_value_weight, preferred_element_type=jnp.float32)
    down_all, up_all = (
        lax.all_gather(adapter_down_maps, "req", axis=0, tiled=True),
        lax.all_gather(adapter_up_maps, "req", axis=0, tiled=True),
    )
    block_total = group_rows // BLOCK
    chosen_down = down_all[adapter_per_block]
    chosen_up = up_all[adapter_per_block]
    block_grouped = hidden.reshape(block_total, BLOCK, local_width)
    reduced_part = jnp.einsum(
        "uqo,uop->uqp", block_grouped, chosen_down, preferred_element_type=jnp.float32
    )
    reduced_rank = lax.psum(reduced_part, "tp").astype(jnp.bfloat16)
    adapter_term = jnp.einsum(
        "epl,elm->epm", reduced_rank, chosen_up, preferred_element_type=jnp.float32
    ).reshape(group_rows, head_cols)
    places = lax.axis_index("req") * group_rows + jnp.arange(group_rows, dtype=jnp.int32)
    positions = places - token_request_start * BLOCK
    complete_query = query_total + ADAPTER_SCALE * adapter_term
    kv_piece = kv_sum.astype(jnp.bfloat16)
    head_block = kv_piece
    for bit_number in range(spread.bit_length() - 1):
        partner = from_partner(head_block, "tp", bit_number)
        upper_side = device // 2**bit_number % 2
        head_block = jnp.where(
            upper_side == 1,
            jnp.concatenate([partner, head_block], axis=1),
            jnp.concatenate([head_block, partner], axis=1),
        )
    key_rows = rotate(head_block[:, :HEAD_SIZE].astype(jnp.float32), positions).astype(jnp.bfloat16)
    value_rows = head_block[:, HEAD_SIZE:]
    head_query = rotate(complete_query, positions).astype(jnp.bfloat16)
    outputs = attend(head_query, key_rows, value_rows, token_request_start)
    return outputs


def solution(mesh):
    in_specs = (
        P("req", "tp"),
        P(None, "tp"),
        P(None, "tp"),
        P("req", "tp", None),
        P("req", None, "tp"),
        P("req"),
        P("req"),
    )
    out_specs = P("req", "tp")
    return jax.shard_map(body, mesh=mesh, in_specs=in_specs, out_specs=out_specs, check_vma=False)
```

profile of v0, /device:TPU:4, one launch (start us, length us, event | category | flops | bytes accessed | tf_op | source)
XLA Modules:
  0.0 415.5 jit_solution(10693275927732517615)
XLA Ops:
  6.5 0.7 all-gather.2.cloned.1.call-update
  7.3 0.7 compare_select_fusion
  8.0 8.5 %all_gather.10 = bf16[64,128,32]{1,2,0:T(8,128)(2,1)S(1)} all-gather(bf16[16,128,32]{1,2,0:T(8,128)(2,1)} %param.12), channel_id=1, replica_groups=mesh['req'=4,'tp'=64] {'req'}, dimensions={0}, use_global_device_ids=true | all-gather | bytes 655360 | tf_op jit(solution)/shard_map/all_gather | solution.py:85
  17.0 1.2 convolution_bitcast_fusion
  18.2 11.8 %all_gather.11 = bf16[64,32,128]{2,1,0:T(8,128)(2,1)S(1)} all-gather(bf16[16,32,128]{2,1,0:T(8,128)(2,1)} %param.13), channel_id=1, replica_groups=mesh['req'=4,'tp'=64] {'req'}, dimensions={0}, use_global_device_ids=true | all-gather | bytes 655360 | tf_op jit(solution)/shard_map/all_gather | solution.py:86
  30.6 314.2 %all-reduce.1 = bf16[8,128,32]{1,2,0:T(8,128)(2,1)S(1)} all-reduce(f32[8,128,32]{1,2,0:T(8,128)S(1)} %convolution_bitcast_fusion), channel_id=1, replica_groups=mesh['req'=4,'tp'=64] {'tp'}, use_global_device_ids=true, to_apply=%region_0.0 | all-reduce | flops 32768 | bytes 196608 | tf_op jit(solution)/shard_map/psum | solution.py:95
  344.8 13.7 %all-gather.2.cloned.1.call-done = bf16[1024,8192]{1,0:T(8,128)(2,1)} async-done(((bf16[1024,128]{1,0:T(8,128)(2,1)}), bf16[1024,8192]{1,0:T(8,128)(2,1)}) %all-gather.2.cloned.1.call-update) | async-done | bytes 16777232 | tf_op jit(solution)/shard_map/all_gather | solution.py:81
  358.5 10.8 %convolution_convert_fusion.1 = bf16[1024,32]{0,1:T(8,128)(2,1)S(1)} fusion(bf16[1024,8192]{1,0:T(8,128)(2,1)} %all-gather.2.cloned.1.call-done, bf16[8192,32]{0,1:T(8,128)(2,1)S(1)} %copy-done.1), kind=kOutput, calls=%fused_computation.14 | convolution fusion | flops 536903680 | bytes 17367040 | tf_op jit(solution)/shard_map/dot_general | solution.py:83
  370.2 3.5 collective-permute-done
  373.7 6.2 %collective-permute-start.1 = (bf16[1024,64]{0,1:T(8,128)(2,1)S(1)}, bf16[1024,64]{0,1:T(8,128)(2,1)}, u32[]{:S(2)}, u32[]{:S(2)}) collective-permute-start(bf16[1024,64]{0,1:T(8,128)(2,1)S(1)} %maximum_select_fusion.2), channel_id=1, source_target_pairs={{0,2},{2,0},{1,3},{3,1},{4,6},{6,4},{5,7},{7,5},{8,10},{10,8},{9,1... | collective-permute-start | bytes 393224 | tf_op jit(solution)/shard_map/ppermute | solution.py:20
  380.0 2.8 collective-permute-done.1
  382.9 1.0 maximum_select_fusion.1
  383.9 3.0 collective-permute-start.2
  386.9 11.4 %convolution_add_fusion = f32[1024,128]{0,1:T(8,128)S(1)} fusion(f32[1024,128]{0,1:T(8,128)S(1)} %copy.16, bf16[1024,8192]{1,0:T(8,128)(2,1)} %all-gather.2.cloned.1.call-done, bf16[8192,128]{1,0:T(8,128)(2,1)S(1)} %copy-done), kind=kOutput, calls=%fused_computation.12 | convolution fusion | flops 2147614720 | bytes 19922944 | tf_op jit(solution)/shard_map/dot_general | solution.py:82
  398.3 1.2 maximum_select_fusion
  399.6 1.2 fusion.18
  401.3 6.7 %while.11 = (s32[]{:T(128)}, bf16[2,512,128]{2,1,0:T(8,128)(2,1)S(1)}, s32[2]{0:T(128)S(1)}, s32[1024]{0:T(1024)S(1)}, s32[1024]{0:T(1024)S(1)}, /*index=5*/bf16...) while((s32[]{:T(128)}, ...), condition=%wide.region_4.5_spmd.clone, body=%wide.region_1.4_spmd.clone.sunk | while | flops 274267136 | bytes 7108799 | solution.py:62
  401.3 0.6 dynamic_slice.26
  402.7 0.8 fusion.41
  404.0 0.6 fusion.43
  404.6 0.6 dynamic_slice.26
  406.0 0.8 fusion.41
  407.3 0.6 fusion.43
  408.0 0.7 copy-done.4
  (33 shorter events, 4.0 us)
Async XLA Ops:
  6.5 380.4 %copy-start = (bf16[8192,128]{1,0:T(8,128)(2,1)S(1)}, bf16[8192,128]{1,0:T(8,128)(2,1)}, u32[]{:S(2)}) copy-start(bf16[8192,128]{1,0:T(8,128)(2,1)} %param.10) | copy-start | bytes 6291460
  6.5 352.0 %copy-start.1 = (bf16[8192,32]{0,1:T(8,128)(2,1)S(1)}, bf16[8192,32]{0,1:T(8,128)(2,1)}, u32[]{:S(2)}) copy-start(bf16[8192,32]{0,1:T(8,128)(2,1)} %param.11) | copy-start | bytes 1572868
  6.5 352.0 %all-gather.2.cloned.1.call-start = ((), (), s32[]{:S(2)}) async-start(), calls=%async_computation | async-start | bytes 17039360 | tf_op jit(solution)/shard_map/all_gather | solution.py:81
  344.8 35.0 %copy-start.2 = (s32[1024]{0:T(1024)S(1)}, s32[1024]{0:T(1024)}, u32[]{:S(2)}) copy-start(s32[1024]{0:T(1024)} %param.14) | copy-start | bytes 12292
  369.3 4.3 %collective-permute-start = (bf16[1024,32]{0,1:T(8,128)(2,1)S(1)}, bf16[1024,32]{0,1:T(8,128)(2,1)S(1)}, u32[]{:S(2)}, u32[]{:S(2)}) collective-permute-start(bf16[1024,32]{0,1:T(8,128)(2,1)S(1)} %convolution_convert_fusion.1), channel_id=1, source_target_pairs={{0,1},{1,0},{2,3},{3,2},{4,5},{5,4},{6,7},{7,6},{8,9},{9,8},{10,11... | collective-permute-start | bytes 196616 | tf_op jit(solution)/shard_map/ppermute | solution.py:20
  373.7 9.2 %collective-permute-start.1 = (bf16[1024,64]{0,1:T(8,128)(2,1)S(1)}, bf16[1024,64]{0,1:T(8,128)(2,1)}, u32[]{:S(2)}, u32[]{:S(2)}) collective-permute-start(bf16[1024,64]{0,1:T(8,128)(2,1)S(1)} %maximum_select_fusion.2), channel_id=1, source_target_pairs={{0,2},{2,0},{1,3},{3,1},{4,6},{6,4},{5,7},{7,5},{8,10},{10,8},{9,1... | collective-permute-start | bytes 393224 | tf_op jit(solution)/shard_map/ppermute | solution.py:20
  383.9 14.4 %collective-permute-start.2 = (bf16[1024,128]{0,1:T(8,128)(2,1)S(1)}, bf16[1024,128]{0,1:T(8,128)(2,1)}, u32[]{:S(2)}, u32[]{:S(2)}) collective-permute-start(bf16[1024,128]{0,1:T(8,128)(2,1)S(1)} %maximum_select_fusion.1), channel_id=1, source_target_pairs={{0,4},{4,0},{1,5},{5,1},{2,6},{6,2},{3,7},{7,3},{8,12},{12,8},{9,1... | collective-permute-start | bytes 786440 | tf_op jit(solution)/shard_map/ppermute | solution.py:20
  399.6 1.7 copy-start.3
  408.0 0.7 copy-start.4
Sparse Core Ops, SparseCore 0:
  9.1 349.3 all-gather.1
where the time goes:
time: 416 us
  blocking collectives  335 us (81%)
  matrix products  26.5 us (6%)
  waiting for transfers between devices  20.7 us (5%)
  between operations  13.6 us (3%)
  starting transfers between devices  9.68 us (2%)
  other arithmetic  5.36 us (1%)
    psum x1, blocking collectives, body(): reduced_rank = lax.psum(reduced_part, 'tp').astype(jnp.bfloat16)  314 us
    all_gather x1, waiting for transfers between devices, body(): piece = lax.all_gather(hidden, 'tp', axis=1, tiled=True)  13.7 us
    all_gather x1, blocking collectives, body(): lax.all_gather(adapter_up_maps, 'req', axis=0, tiled=True)  11.8 us
    dot_general x1, matrix products, body(): jnp.dot(piece, query_weight, preferred_element_type=jnp.float32)  11.4 us
    dot_general x1, matrix products, body(): jnp.dot(piece, key_value_weight, preferred_element_type=jnp.float32)  10.8 us
    ppermute x3, starting transfers between devices, from_partner(): return lax.ppermute(block, axis, route)  9.68 us
    all_gather x1, blocking collectives, body(): lax.all_gather(adapter_down_maps, 'req', axis=0, tiled=True)  8.48 us
  transfers between devices with their start and end apart: 4, of which 3 were waited for; matrix products, arithmetic and copies ran while one was open for 4% of the time, Pallas kernels for 0%

commit v1 on v0

--- a/solution.py
+++ b/solution.py
@@ -82,7 +82,10 @@
     query_total = jnp.dot(piece, query_weight, preferred_element_type=jnp.float32)
     kv_sum = jnp.dot(piece, key_value_weight, preferred_element_type=jnp.float32)
     down_all, up_all = (
-        lax.all_gather(adapter_down_maps, "req", axis=0, tiled=True),
+        jnp.concatenate(
+            lax.all_to_all(jnp.stack([adapter_down_maps] * lax.axis_size("req")), "req", 0, 0),
+            axis=0,
+        ),
         lax.all_gather(adapter_up_maps, "req", axis=0, tiled=True),
     )
     block_total = group_rows // BLOCK

time: 416 us -> 715 us (1.72)
  waiting for transfers between devices: 20.7 us -> 337 us
  blocking collectives: 335 us -> 318 us
    all_gather x1, waiting for transfers between devices: 13.7 us -> 331 us  [body(): piece = lax.all_gather(hidden, 'tp', axis=1, tiled=True)]
    all_gather x1 -> x0, blocking collectives: 8.48 us -> none  [body(): lax.all_gather(adapter_down_maps, 'req', axis=0, tiled=True)]
    ppermute x3, starting transfers between devices: 9.68 us -> 2.08 us  [from_partner(): return lax.ppermute(block, axis, route)]
    psum x1, blocking collectives: 314 us -> 307 us  [body(): reduced_rank = lax.psum(reduced_part, 'tp').astype(jnp.bfloat16)]
  transfers between devices with their start and end apart: 4 -> 5, of which waited for: 3 -> 2; matrix products, arithmetic and copies ran while one was open for 4% -> 2% of each run, Pallas kernels for 0% -> 0%
where the time goes in v1:
time: 715 us; the launch traced here: 714 us
  waiting for transfers between devices  337 us (47%)
  blocking collectives  318 us (44%)
  matrix products  25.6 us (4%)
  between operations  13.6 us (2%)
  starting transfers between devices  7.8 us (1%)
    all_gather x1, waiting for transfers between devices, body(): piece = lax.all_gather(hidden, 'tp', axis=1, tiled=True)  331 us
    psum x1, blocking collectives, body(): reduced_rank = lax.psum(reduced_part, 'tp').astype(jnp.bfloat16)  307 us
  transfers between devices with their start and end apart: 5, of which 2 were waited for; matrix products, arithmetic and copies ran while one was open for 2% of the time, Pallas kernels for 0%

profile of v1, /device:TPU:4, one launch (start us, length us, event | category | flops | bytes accessed | tf_op | source)
XLA Modules:
  0.0 714.4 jit_solution(6484012440040664613)
XLA Ops:
  6.6 0.7 all-gather.2.cloned.1.call-update
  7.3 1.9 stack.2
  9.1 5.7 all-to-all-start
  14.8 10.8 %all_gather.7 = bf16[64,32,128]{2,1,0:T(8,128)(2,1)S(1)} all-gather(bf16[16,32,128]{2,1,0:T(8,128)(2,1)S(1)} %copy-done.3), channel_id=1, replica_groups=mesh['req'=4,'tp'=64] {'req'}, dimensions={0}, use_global_device_ids=true | all-gather | bytes 655360 | tf_op jit(solution)/shard_map/all_gather | solution.py:89
  25.7 1.2 gather_fusion.1
  26.9 0.6 gather_fusion
  27.7 330.6 %all-gather.2.cloned.1.call-done = bf16[1024,8192]{1,0:T(8,128)(2,1)} async-done(((bf16[1024,128]{1,0:T(8,128)(2,1)}), bf16[1024,8192]{1,0:T(8,128)(2,1)}) %all-gather.2.cloned.1.call-update) | async-done | bytes 16777232 | tf_op jit(solution)/shard_map/all_gather | solution.py:81
  358.4 10.9 %convolution_convert_fusion.1 = bf16[1024,32]{0,1:T(8,128)(2,1)S(1)} fusion(bf16[1024,8192]{1,0:T(8,128)(2,1)} %all-gather.2.cloned.1.call-done, bf16[8192,32]{0,1:T(8,128)(2,1)} %param.11), kind=kOutput, calls=%fused_computation.14 | convolution fusion | flops 536903680 | bytes 17367040 | tf_op jit(solution)/shard_map/dot_general | solution.py:83
  369.2 1.7 collective-permute-start
  370.9 306.8 %all-reduce.1 = bf16[8,128,32]{1,2,0:T(8,128)(2,1)S(1)} all-reduce(f32[8,128,32]{1,2,0:T(8,128)S(1)} %convolution_bitcast_fusion), channel_id=1, replica_groups=mesh['req'=4,'tp'=64] {'tp'}, use_global_device_ids=true, to_apply=%region_0.0 | all-reduce | flops 32768 | bytes 196608 | tf_op jit(solution)/shard_map/psum | solution.py:98
  678.4 6.1 collective-permute-done.1
  684.4 1.0 maximum_select_fusion.1
  685.8 11.4 %convolution_add_fusion = f32[1024,128]{0,1:T(8,128)S(1)} fusion(f32[1024,128]{0,1:T(8,128)S(1)} %copy.17, bf16[1024,8192]{1,0:T(8,128)(2,1)} %all-gather.2.cloned.1.call-done, bf16[8192,128]{1,0:T(8,128)(2,1)S(1)} %copy-done), kind=kOutput, calls=%fused_computation.12 | convolution fusion | flops 2147614720 | bytes 19922944 | tf_op jit(solution)/shard_map/dot_general | solution.py:82
  697.2 1.2 maximum_select_fusion
  698.5 1.2 fusion.18
  700.2 6.7 while.11
  700.2 0.6 dynamic_slice.26
  701.6 0.8 fusion.41
  702.4 0.5 fusion.42
  702.9 0.6 fusion.43
  703.5 0.6 dynamic_slice.26
  704.9 0.8 fusion.41
  706.2 0.6 fusion.43
  706.8 0.7 copy-done.7
  (41 shorter events, 2.5 us)
Async XLA Ops:
  6.5 679.2 %copy-start = (bf16[8192,128]{1,0:T(8,128)(2,1)S(1)}, bf16[8192,128]{1,0:T(8,128)(2,1)}, u32[]{:S(2)}) copy-start(bf16[8192,128]{1,0:T(8,128)(2,1)} %param.10) | copy-start | bytes 6291460
  6.5 20.9 %copy-start.1 = (bf16[1024,128]{1,0:T(8,128)(2,1)S(1)}, bf16[1024,128]{1,0:T(8,128)(2,1)}, u32[]{:S(2)}) copy-start(bf16[1024,128]{1,0:T(8,128)(2,1)} %param.9) | copy-start | bytes 786436
  6.5 8.3 %copy-start.3 = (bf16[16,32,128]{2,1,0:T(8,128)(2,1)S(1)}, bf16[16,32,128]{2,1,0:T(8,128)(2,1)}, u32[]{:S(2)}) copy-start(bf16[16,32,128]{2,1,0:T(8,128)(2,1)} %param.13) | copy-start | bytes 393220
  6.5 19.1 %copy-start.5 = (s32[8]{0:T(128)S(1)}, s32[8]{0:T(128)}, u32[]{:S(2)}) copy-start(s32[8]{0:T(128)} %param.15) | copy-start | bytes 100
  6.5 20.3 %copy-start.4 = (s32[1024]{0:T(1024)S(1)}, s32[1024]{0:T(1024)}, u32[]{:S(2)}) copy-start(s32[1024]{0:T(1024)} %param.14) | copy-start | bytes 12292
  6.5 351.8 %all-gather.2.cloned.1.call-start = ((), (), s32[]{:S(2)}) async-start(), calls=%async_computation.1 | async-start | bytes 17039360 | tf_op jit(solution)/shard_map/all_gather | solution.py:81
  9.1 17.8 %all-to-all-start = ((bf16[4,16,128,32]{2,3,1,0:T(8,128)(2,1)}), bf16[4,16,128,32]{2,3,1,0:T(8,128)(2,1)S(1)}, u32[]{:S(2)}, u32[]{:S(2)}) async-start(bf16[4,16,128,32]{2,3,1,0:T(8,128)(2,1)} %stack.2), calls=%async_computation | async-start | bytes 1048576 | tf_op jit(solution)/shard_map/all_to_all | solution.py:86
  27.7 650.2 %copy-start.2 = (bf16[8,32,128]{2,1,0:T(8,128)(2,1)S(1)}, bf16[8,32,128]{2,1,0:T(8,128)(2,1)}, u32[]{:S(2)}) copy-start(bf16[8,32,128]{2,1,0:T(8,128)(2,1)} %gather_fusion.1) | copy-start | bytes 196612
  369.2 308.5 %collective-permute-start = (bf16[1024,32]{0,1:T(8,128)(2,1)S(1)}, bf16[1024,32]{0,1:T(8,128)(2,1)S(1)}, u32[]{:S(2)}, u32[]{:S(2)}) collective-permute-start(bf16[1024,32]{0,1:T(8,128)(2,1)S(1)} %convolution_convert_fusion.1), channel_id=1, source_target_pairs={{0,1},{1,0},{2,3},{3,2},{4,5},{5,4},{6,7},{7,6},{8,9},{9,8},{10,11... | collective-permute-start | bytes 196616 | tf_op jit(solution)/shard_map/ppermute | solution.py:20
  677.8 6.7 collective-permute-start.1
  685.5 11.7 %collective-permute-start.2 = (bf16[1024,128]{0,1:T(8,128)(2,1)S(1)}, bf16[1024,128]{0,1:T(8,128)(2,1)}, u32[]{:S(2)}, u32[]{:S(2)}) collective-permute-start(bf16[1024,128]{0,1:T(8,128)(2,1)S(1)} %maximum_select_fusion.1), channel_id=1, source_target_pairs={{0,4},{4,0},{1,5},{5,1},{2,6},{6,2},{3,7},{7,3},{8,12},{12,8},{9,1... | collective-permute-start | bytes 786440 | tf_op jit(solution)/shard_map/ppermute | solution.py:20
  698.5 1.7 copy-start.6
  706.8 0.7 copy-start.7
Sparse Core Ops, SparseCore 0:
  9.1 349.2 all-gather.1
